TPU v7x, 32 devices: a whole 2x2x4 slice. The times are simulated.
32 devices in a mesh: space: 8 (over z, core), tm: 4 (over y, x).
Axes of the slice: x: 2, y: 2, z: 4, core: 2. Of those that a mesh axis runs over, the one named last changes fastest.
Arguments:
- snapshots: bfloat16 [32768, 512], P('space', 'tm'), may hold values from -6 to 6
- stencil_starts: int32 [512], P('tm'), may hold values from 0 to 508, as said below
- stencil_widths: int32 [512], P('tm'), may hold values from 4 to 40, as said below
- stencil_coeffs: bfloat16 [512, 40], P('tm'), may hold values from -2 to 2
- panels: bfloat16 [512, 256], P('tm'), may hold values from -0.25 to 0.25
Outputs:
- gram: float32 [512, 512], P(('tm', 'space'))
- modes: bfloat16 [32768, 256], P(('space', 'tm'))
Inputs may be any that keep to these rules, and one draw needn't show every extreme that they name: `stencil_starts`: uniform time u's stencil starts inside its own time block, snapshots from (u // 128) * 128 to that plus 128 - 1, and ends before snapshot 512. `stencil_widths`: some stencil has width 40 and some has width 4.
All inputs are finite; a program needn't handle non-finite values.
Results may differ from a plain program's by a relative error of at most 0.0049.
Values may be sent and summed in bfloat16 or wider, within the bound.
A program may use at most 64 MiB of HBM per device.

v0:
```python
import jax
import jax.numpy as jnp
from jax import lax
from jax.sharding import PartitionSpec as P


def shifted(value, axis, steps):
    count = lax.axis_size(axis)
    initial, last = (max(0, -steps), min(count, count - steps))
    return lax.ppermute(value, axis, [(source, source + steps) for source in range(initial, last)])


def on_device(snapshots, stencil_starts, stencil_widths, stencil_coeffs, panels):
    rows, block = snapshots.shape
    width_max = stencil_coeffs.shape[1]
    rim = shifted(snapshots[:, : width_max - 1], "tm", -1)
    extended = jnp.concatenate([snapshots, rim], axis=1)
    offsets = stencil_starts - lax.axis_index("tm") * block
    position = jnp.arange(block + width_max - 1, dtype=jnp.int32)[:, None]
    relative = position - offsets[None, :]
    steps = jnp.arange(width_max, dtype=jnp.int32)[:, None, None]
    picked = (relative[None, :, :] == steps) & (steps < stencil_widths[None, None, :])
    coeff_table = stencil_coeffs.T[:, None, :].astype(jnp.float32)
    weights = jnp.sum(jnp.where(picked, coeff_table, 0.0), axis=0).astype(jnp.bfloat16)
    resampled = jnp.dot(extended, weights, preferred_element_type=jnp.float32).astype(jnp.bfloat16)
    scale = 1.0 / (rows * lax.axis_size("space"))
    share = rows // lax.axis_size("tm")
    whole = lax.all_gather(resampled, "tm", axis=1, tiled=True)
    partial_value = lax.dot_general(
        resampled, whole, (((0,), (0,)), ((), ())), preferred_element_type=jnp.float32
    )
    every_panel = lax.all_gather(panels, "tm", axis=0, tiled=True)
    mine = lax.dynamic_slice_in_dim(whole, lax.axis_index("tm") * share, share, 0)
    modes = jnp.dot(mine, every_panel, preferred_element_type=jnp.float32).astype(jnp.bfloat16)
    partial_value = partial_value * scale
    gram = lax.psum_scatter(partial_value, "space", scatter_dimension=0, tiled=True)
    return (gram, modes)


def solution(mesh):
    return jax.shard_map(
        on_device,
        mesh=mesh,
        in_specs=(P("space", "tm"), P("tm"), P("tm"), P("tm", None), P("tm", None)),
        out_specs=(P(("tm", "space"), None), P(("space", "tm"), None)),
        check_vma=False,
    )
```

profile of v0, /device:TPU:0, one launch (start us, length us, event | category | flops | bytes accessed | tf_op | source)
XLA Modules:
  0.0 120.7 jit_solution(11758978963417569077)
XLA Ops:
  7.2 0.0 all-gather.2.cloned.1.call-start
  7.2 1.6 %copy.11 = bf16[4096,39]{0,1:T(8,128)(2,1)S(1)} copy(bf16[4096,39]{1,0:T(8,128)(2,1)} %bitcast.7) | data formatting | bytes 638976
  8.8 1.3 %collective-permute-start = (bf16[4096,39]{0,1:T(8,128)(2,1)S(1)}, bf16[4096,39]{0,1:T(8,128)(2,1)S(1)}, u32[]{:S(2)}, u32[]{:S(2)}) collective-permute-start(bf16[4096,39]{0,1:T(8,128)(2,1)S(1)} %copy.11), channel_id=1, source_target_pairs={{1,0},{2,1},{3,2},{5,4},{6,5},{7,6},{9,8},{10,9},{11,10},{13,12},{... | collective-permute-start | bytes 958472 | tf_op jit(solution)/shard_map/ppermute | solution.py:10
  10.1 0.7 convert_bitcast_fusion
  10.8 0.7 broadcast_subtract_fusion
  11.5 0.7 iota_compare_fusion.1
  12.2 1.4 %select_reduce_fusion = bf16[167,128]{1,0:T(8,128)(2,1)S(1)} fusion(f32[40,128]{1,0:T(8,128)S(1)} %convert_bitcast_fusion, s32[167,128]{1,0:T(8,128)S(1)} %iota_subtract_fusion, pred[40,128]{1,0:T(8,128)(4,1)S(1)} %iota_compare_fusion.1), kind=kLoop, calls=%fused_computation.1 | loop fusion | flops 3398784 | bytes 153856 | tf_op jit(solution)/shard_map/reduce_sum | solution.py:24
  13.6 7.8 %collective-permute-done = bf16[4096,39]{0,1:T(8,128)(2,1)S(1)} collective-permute-done((bf16[4096,39]{0,1:T(8,128)(2,1)S(1)}, bf16[4096,39]{0,1:T(8,128)(2,1)S(1)}, u32[]{:S(2)}, u32[]{:S(2)}) %collective-permute-start) | collective-permute-done | bytes 319520 | tf_op jit(solution)/shard_map/ppermute | solution.py:10
  21.4 0.5 copy.10
  21.9 2.9 %convolution_convert_fusion = bf16[4096,128]{1,0:T(8,128)(2,1)} fusion(bf16[4096,39]{1,0:T(8,128)(2,1)S(1)} %copy.10, bf16[4096,128]{1,0:T(8,128)(2,1)} %param.5, bf16[167,128]{1,0:T(8,128)(2,1)S(1)} %select_reduce_fusion), kind=kOutput, calls=%fused_computation | convolution fusion | flops 178372608 | bytes 2459392 | tf_op jit(solution)/shard_map/dot_general | solution.py:25
  24.8 0.0 copy-start
  24.8 0.0 all-gather.2.cloned.1.call-update
  24.8 0.0 reduce-scatter.2.cloned.1.call-start
  24.9 54.0 %all-gather.2.cloned.1.call-done = bf16[4096,512]{1,0:T(8,128)(2,1)} async-done(((bf16[4096,128]{1,0:T(8,128)(2,1)}), bf16[4096,512]{1,0:T(8,128)(2,1)}) %all-gather.2.cloned.1.call-update) | async-done | bytes 4194320 | tf_op jit(solution)/shard_map/all_gather | solution.py:28
  78.9 4.0 %convolution_multiply_fusion = f32[128,512]{1,0:T(8,128)} fusion(bf16[4096,128]{1,0:T(8,128)(2,1)} %convolution_convert_fusion, bf16[4096,512]{1,0:T(8,128)(2,1)} %all-gather.2.cloned.1.call-done), kind=kOutput, calls=%fused_computation.8 | convolution fusion | flops 536936448 | bytes 5505024 | tf_op jit(solution)/shard_map/dot_general | solution.py:29
  82.8 0.0 reduce-scatter.2.cloned.1.call-update
  82.9 0.0 copy-done
  82.9 9.0 %all_gather.7 = bf16[512,256]{1,0:T(8,128)(2,1)S(1)} all-gather(bf16[128,256]{1,0:T(8,128)(2,1)S(1)} %copy-done), channel_id=1, replica_groups=mesh['space'=8,'tm'=4] {'tm'}, dimensions={0}, use_global_device_ids=true | all-gather | bytes 327680 | tf_op jit(solution)/shard_map/all_gather | solution.py:32
  91.9 2.5 %convolution_convert_fusion.1 = bf16[1024,256]{1,0:T(8,128)(2,1)} fusion(bf16[512,256]{1,0:T(8,128)(2,1)S(1)} %all_gather.7, bf16[4096,512]{1,0:T(8,128)(2,1)} %all-gather.2.cloned.1.call-done, s32[]{:T(128)S(6)} %select_n.8), kind=kOutput, calls=%fused_computation.7 | convolution fusion | flops 268697600 | bytes 1835012 | tf_op jit(solution)/shard_map/dot_general | solution.py:34
  94.3 19.6 %reduce-scatter.2.cloned.1.call-done = f32[16,512]{1,0:T(8,128)} async-done(((f32[128,512]{1,0:T(8,128)}), f32[16,512]{1,0:T(8,128)}) %reduce-scatter.2.cloned.1.call-update) | async-done | bytes 32784 | tf_op jit(solution)/shard_map/reduce_scatter | solution.py:36
  (1 shorter events, 0.0 us)
Async XLA Ops:
  7.2 71.7 %all-gather.2.cloned.1.call-start = ((), (), s32[]{:S(2)}) async-start(), calls=%async_computation.1 | async-start | bytes 5242880 | tf_op jit(solution)/shard_map/all_gather | solution.py:28
  8.8 12.6 %collective-permute-start = (bf16[4096,39]{0,1:T(8,128)(2,1)S(1)}, bf16[4096,39]{0,1:T(8,128)(2,1)S(1)}, u32[]{:S(2)}, u32[]{:S(2)}) collective-permute-start(bf16[4096,39]{0,1:T(8,128)(2,1)S(1)} %copy.11), channel_id=1, source_target_pairs={{1,0},{2,1},{3,2},{5,4},{6,5},{7,6},{9,8},{10,9},{11,10},{13,12},{... | collective-permute-start | bytes 958472 | tf_op jit(solution)/shard_map/ppermute | solution.py:10
  24.8 58.1 %copy-start = (bf16[128,256]{1,0:T(8,128)(2,1)S(1)}, bf16[128,256]{1,0:T(8,128)(2,1)}, u32[]{:S(2)}) copy-start(bf16[128,256]{1,0:T(8,128)(2,1)} %param.9) | copy-start | bytes 196612
  24.8 89.1 %reduce-scatter.2.cloned.1.call-start = ((), (), s32[]{:S(2)}) async-start(), calls=%async_computation.2 | async-start | bytes 294912 | tf_op jit(solution)/shard_map/reduce_scatter | solution.py:36
Sparse Core Ops, SparseCore 0:
  24.9 53.8 all-gather.1
  83.0 30.8 reduce-scatter.1
where the time goes:
time: 121 us
  waiting for transfers between devices  81.4 us (67%)
  between operations  14.1 us (12%)
  matrix products  9.31 us (8%)
  blocking collectives  9 us (7%)
  other arithmetic  3.49 us (3%)
  local copies, waits for them, and re-layouts  2.12 us (2%)
  starting transfers between devices  1.36 us (1%)
    all_gather x1, waiting for transfers between devices, on_device(): whole = lax.all_gather(resampled, 'tm', axis=1, tiled=True)  54 us
    reduce_scatter x1, waiting for transfers between devices, on_device(): lax.psum_scatter(partial_value, 'space', scatter_dimension=0, tiled=True)  19.6 us
    all_gather x1, blocking collectives, on_device(): every_panel = lax.all_gather(panels, 'tm', axis=0, tiled=True)  9 us
    ppermute x1, waiting for transfers between devices, shifted(): lax.ppermute(value, axis, [(source, source + steps) for source in range(i...  7.78 us
    dot_general x1, matrix products, on_device(): lax.dot_general(resampled, whole, (((0,), (0,)), ((), ())), preferred_ele...  3.97 us
    dot_general x1, matrix products, on_device(): jnp.dot(extended, weights, preferred_element_type=jnp.float32)  2.9 us
    dot_general x1, matrix products, on_device(): jnp.dot(mine, every_panel, preferred_element_type=jnp.float32)  2.45 us
  transfers between devices with their start and end apart: 3, of which 3 were waited for; matrix products, arithmetic and copies ran while one was open for 5% of the time, Pallas kernels for 0%

commit v1 on v0

--- a/solution.py
+++ b/solution.py
@@ -25,7 +25,15 @@
     resampled = jnp.dot(extended, weights, preferred_element_type=jnp.float32).astype(jnp.bfloat16)
     scale = 1.0 / (rows * lax.axis_size("space"))
     share = rows // lax.axis_size("tm")
-    whole = lax.all_gather(resampled, "tm", axis=1, tiled=True)
+    ways, here = (lax.axis_size("tm"), lax.axis_index("tm"))
+    grown, reach = (resampled, 1)
+    while reach < ways:
+        theirs = lax.ppermute(grown, "tm", [(d, d ^ reach) for d in range(ways)])
+        mine_first = jnp.concatenate([grown, theirs], axis=1)
+        theirs_first = jnp.concatenate([theirs, grown], axis=1)
+        grown = jnp.where(here & reach == 0, mine_first, theirs_first)
+        reach = 2 * reach
+    whole = grown
     partial_value = lax.dot_general(
         resampled, whole, (((0,), (0,)), ((), ())), preferred_element_type=jnp.float32
     )

time: 121 us -> 143 us (1.18)
  waiting for transfers between devices: 81.4 us -> 95 us
  other arithmetic: 3.49 us -> 9.06 us
  starting transfers between devices: 1.36 us -> 4.95 us
  matrix products: 9.31 us -> 6.84 us
  local copies, waits for them, and re-layouts: 2.12 us -> 4.05 us
    ppermute x0 -> x2, waiting for transfers between devices: none -> 67.6 us  [on_device(): theirs = lax.ppermute(grown, 'tm', [(d, d ^ reach) for d in range(ways)])]
    all_gather x1 -> x0, waiting for transfers between devices: 54 us -> none  [on_device(): whole = lax.all_gather(resampled, 'tm', axis=1, tiled=True)]
    select_n x0 -> x2, other arithmetic: none -> 5.57 us  [on_device(): grown = jnp.where(here & reach == 0, mine_first, theirs_first)]
    ppermute x0 -> x2, starting transfers between devices: none -> 3.63 us  [on_device(): theirs = lax.ppermute(grown, 'tm', [(d, d ^ reach) for d in range(ways)])]
    unnamed x3 -> x5, local copies, waits for them, and re-layouts: 1.63 us -> 3.55 us
    dot_general x1, matrix products: 3.97 us -> 2.28 us  [on_device(): lax.dot_general(resampled, whole, (((0,), (0,)), ((), ())), preferred_ele...]
  transfers between devices with their start and end apart: 3 -> 4, of which waited for: 3 -> 4; matrix products, arithmetic and copies ran while one was open for 5% -> 4% of each run, Pallas kernels for 0% -> 0%
where the time goes in v1:
time: 143 us
  waiting for transfers between devices  95 us (66%)
  between operations  14.1 us (10%)
  other arithmetic  9.06 us (6%)
  blocking collectives  8.93 us (6%)
  matrix products  6.84 us (5%)
  starting transfers between devices  4.95 us (3%)
  local copies, waits for them, and re-layouts  4.05 us (3%)
    ppermute x2, waiting for transfers between devices, on_device(): theirs = lax.ppermute(grown, 'tm', [(d, d ^ reach) for d in range(ways)])  67.6 us
    reduce_scatter x1, waiting for transfers between devices, on_device(): lax.psum_scatter(partial_value, 'space', scatter_dimension=0, tiled=True)  19.6 us
    all_gather x1, blocking collectives, on_device(): every_panel = lax.all_gather(panels, 'tm', axis=0, tiled=True)  8.93 us
    ppermute x1, waiting for transfers between devices, shifted(): lax.ppermute(value, axis, [(source, source + steps) for source in range(i...  7.78 us
    select_n x2, other arithmetic, on_device(): grown = jnp.where(here & reach == 0, mine_first, theirs_first)  5.57 us
    ppermute x2, starting transfers between devices, on_device(): theirs = lax.ppermute(grown, 'tm', [(d, d ^ reach) for d in range(ways)])  3.63 us
    unnamed x5, local copies, waits for them, and re-layouts  3.55 us
  transfers between devices with their start and end apart: 4, of which 4 were waited for; matrix products, arithmetic and copies ran while one was open for 4% of the time, Pallas kernels for 0%

profile of v1, /device:TPU:0, one launch (start us, length us, event | category | flops | bytes accessed | tf_op | source)
XLA Modules:
  0.0 142.9 jit_solution(2327150253919211594)
XLA Ops:
  7.2 0.0 reduce-scatter.2.cloned.1.call-start
  7.2 1.6 %copy.11 = bf16[4096,39]{0,1:T(8,128)(2,1)S(1)} copy(bf16[4096,39]{1,0:T(8,128)(2,1)} %bitcast.7) | data formatting | bytes 638976
  8.8 1.3 collective-permute-start
  10.1 0.7 broadcast_subtract_fusion
  10.8 0.7 convert_bitcast_fusion
  11.5 0.7 iota_compare_fusion.1
  12.2 1.4 %select_reduce_fusion = bf16[167,128]{1,0:T(8,128)(2,1)S(1)} fusion(f32[40,128]{1,0:T(8,128)S(1)} %convert_bitcast_fusion, s32[167,128]{1,0:T(8,128)S(1)} %iota_subtract_fusion, pred[40,128]{1,0:T(8,128)(4,1)S(1)} %iota_compare_fusion.1), kind=kLoop, calls=%fused_computation.2 | loop fusion | flops 3398784 | bytes 153856 | tf_op jit(solution)/shard_map/reduce_sum | solution.py:24
  13.6 7.8 %collective-permute-done = bf16[4096,39]{0,1:T(8,128)(2,1)S(1)} collective-permute-done((bf16[4096,39]{0,1:T(8,128)(2,1)S(1)}, bf16[4096,39]{0,1:T(8,128)(2,1)S(1)}, u32[]{:S(2)}, u32[]{:S(2)}) %collective-permute-start) | collective-permute-done | bytes 319520 | tf_op jit(solution)/shard_map/ppermute | solution.py:10
  21.4 0.5 copy.10
  21.9 2.0 %convolution_convert_fusion = bf16[4096,128]{0,1:T(8,128)(2,1)S(1)} fusion(bf16[4096,39]{1,0:T(8,128)(2,1)S(1)} %copy.10, bf16[4096,128]{1,0:T(8,128)(2,1)} %param.5, bf16[167,128]{1,0:T(8,128)(2,1)S(1)} %select_reduce_fusion), kind=kOutput, calls=%fused_computation | convolution fusion | flops 178372608 | bytes 2459392 | tf_op jit(solution)/shard_map/dot_general | solution.py:25
  23.9 2.7 %collective-permute-start.1 = (bf16[4096,128]{0,1:T(8,128)(2,1)S(1)}, bf16[4096,128]{0,1:T(8,128)(2,1)}, u32[]{:S(2)}, u32[]{:S(2)}) collective-permute-start(bf16[4096,128]{0,1:T(8,128)(2,1)S(1)} %convolution_convert_fusion), channel_id=1, source_target_pairs={{0,1},{1,0},{2,3},{3,2},{4,5},{5,4},{6,7},{7,6},{8,9},{9,8},{10,11... | collective-permute-start | bytes 3145736 | tf_op jit(solution)/shard_map/ppermute | solution.py:31
  26.6 22.4 %collective-permute-done.1 = bf16[4096,128]{0,1:T(8,128)(2,1)} collective-permute-done((bf16[4096,128]{0,1:T(8,128)(2,1)S(1)}, bf16[4096,128]{0,1:T(8,128)(2,1)}, u32[]{:S(2)}, u32[]{:S(2)}) %collective-permute-start.1) | collective-permute-done | bytes 1048608 | tf_op jit(solution)/shard_map/ppermute | solution.py:31
  49.1 2.3 %maximum_select_fusion.1 = bf16[4096,256]{0,1:T(8,128)(2,1)S(1)} fusion(bf16[4096,128]{0,1:T(8,128)(2,1)} %collective-permute-done.1, bf16[4096,128]{0,1:T(8,128)(2,1)S(1)} %convolution_convert_fusion, pred[]{:T(512)S(6)} %eq.23), kind=kLoop, calls=%fused_computation.8 | loop fusion | flops 9437184 | bytes 4194305 | tf_op jit(solution)/shard_map/jit(_where)/select_n | solution.py:34
  51.3 0.9 collective-permute-start.2
  52.3 45.2 %collective-permute-done.2 = bf16[4096,256]{0,1:T(8,128)(2,1)} collective-permute-done((bf16[4096,256]{0,1:T(8,128)(2,1)S(1)}, bf16[4096,256]{0,1:T(8,128)(2,1)}, u32[]{:S(2)}, u32[]{:S(2)}) %collective-permute-start.2) | collective-permute-done | bytes 2097184 | tf_op jit(solution)/shard_map/ppermute | solution.py:31
  97.4 3.3 %maximum_select_fusion = bf16[4096,512]{0,1:T(8,128)(2,1)S(1)} fusion(bf16[4096,256]{0,1:T(8,128)(2,1)} %collective-permute-done.2, bf16[4096,256]{0,1:T(8,128)(2,1)S(1)} %maximum_select_fusion.1, pred[]{:T(512)S(6)} %eq.22), kind=kLoop, calls=%fused_computation.1 | loop fusion | flops 18874368 | bytes 8388609 | tf_op jit(solution)/shard_map/jit(_where)/select_n | solution.py:34
  100.7 0.0 copy-start
  100.8 1.9 %copy-done = bf16[4096,512]{0,1:T(8,128)(2,1)} copy-done((bf16[4096,512]{0,1:T(8,128)(2,1)}, bf16[4096,512]{0,1:T(8,128)(2,1)S(1)}, u32[]{:S(2)}) %copy-start) | copy-done | bytes 4194328
  102.7 0.0 copy-start.1
  102.7 2.3 %convolution_multiply_fusion = f32[128,512]{1,0:T(8,128)} fusion(bf16[4096,128]{0,1:T(8,128)(2,1)S(1)} %convolution_convert_fusion, bf16[4096,512]{0,1:T(8,128)(2,1)S(1)} %maximum_select_fusion), kind=kOutput, calls=%fused_computation.10 | convolution fusion | flops 536936448 | bytes 5505024 | tf_op jit(solution)/shard_map/dot_general | solution.py:37
  105.0 0.0 reduce-scatter.2.cloned.1.call-update
  105.0 0.0 copy-done.1
  105.0 8.9 %all_gather.3 = bf16[512,256]{1,0:T(8,128)(2,1)S(1)} all-gather(bf16[128,256]{1,0:T(8,128)(2,1)S(1)} %copy-done.1), channel_id=1, replica_groups=mesh['space'=8,'tm'=4] {'tm'}, dimensions={0}, use_global_device_ids=true | all-gather | bytes 327680 | tf_op jit(solution)/shard_map/all_gather | solution.py:40
  113.9 2.5 %convolution_convert_fusion.1 = bf16[1024,256]{1,0:T(8,128)(2,1)} fusion(bf16[512,256]{1,0:T(8,128)(2,1)S(1)} %all_gather.3, bf16[4096,512]{0,1:T(8,128)(2,1)} %copy-done, s32[]{:T(128)S(6)} %select_n.28), kind=kOutput, calls=%fused_computation.9 | convolution fusion | flops 268697600 | bytes 1835012 | tf_op jit(solution)/shard_map/dot_general | solution.py:42
  116.4 19.6 %reduce-scatter.2.cloned.1.call-done = f32[16,512]{1,0:T(8,128)} async-done(((f32[128,512]{1,0:T(8,128)}), f32[16,512]{1,0:T(8,128)}) %reduce-scatter.2.cloned.1.call-update) | async-done | bytes 32784 | tf_op jit(solution)/shard_map/reduce_scatter | solution.py:44
  (1 shorter events, 0.0 us)
Async XLA Ops:
  7.2 128.9 %reduce-scatter.2.cloned.1.call-start = ((), (), s32[]{:S(2)}) async-start(), calls=%async_computation.1 | async-start | bytes 294912 | tf_op jit(solution)/shard_map/reduce_scatter | solution.py:44
  8.8 12.6 %collective-permute-start = (bf16[4096,39]{0,1:T(8,128)(2,1)S(1)}, bf16[4096,39]{0,1:T(8,128)(2,1)S(1)}, u32[]{:S(2)}, u32[]{:S(2)}) collective-permute-start(bf16[4096,39]{0,1:T(8,128)(2,1)S(1)} %copy.11), channel_id=1, source_target_pairs={{1,0},{2,1},{3,2},{5,4},{6,5},{7,6},{9,8},{10,9},{11,10},{13,12},{... | collective-permute-start | bytes 958472 | tf_op jit(solution)/shard_map/ppermute | solution.py:10
  23.9 25.1 %collective-permute-start.1 = (bf16[4096,128]{0,1:T(8,128)(2,1)S(1)}, bf16[4096,128]{0,1:T(8,128)(2,1)}, u32[]{:S(2)}, u32[]{:S(2)}) collective-permute-start(bf16[4096,128]{0,1:T(8,128)(2,1)S(1)} %convolution_convert_fusion), channel_id=1, source_target_pairs={{0,1},{1,0},{2,3},{3,2},{4,5},{5,4},{6,7},{7,6},{8,9},{9,8},{10,11... | collective-permute-start | bytes 3145736 | tf_op jit(solution)/shard_map/ppermute | solution.py:31
  51.3 46.1 %collective-permute-start.2 = (bf16[4096,256]{0,1:T(8,128)(2,1)S(1)}, bf16[4096,256]{0,1:T(8,128)(2,1)}, u32[]{:S(2)}, u32[]{:S(2)}) collective-permute-start(bf16[4096,256]{0,1:T(8,128)(2,1)S(1)} %maximum_select_fusion.1), channel_id=1, source_target_pairs={{0,2},{1,3},{2,0},{3,1},{4,6},{5,7},{6,4},{7,5},{8,10},{9,11},{10,... | collective-permute-start | bytes 6291464 | tf_op jit(solution)/shard_map/ppermute | solution.py:31
  100.7 1.9 %copy-start = (bf16[4096,512]{0,1:T(8,128)(2,1)}, bf16[4096,512]{0,1:T(8,128)(2,1)S(1)}, u32[]{:S(2)}) copy-start(bf16[4096,512]{0,1:T(8,128)(2,1)S(1)} %maximum_select_fusion) | copy-start | bytes 12582916
  102.7 2.3 %copy-start.1 = (bf16[128,256]{1,0:T(8,128)(2,1)S(1)}, bf16[128,256]{1,0:T(8,128)(2,1)}, u32[]{:S(2)}) copy-start(bf16[128,256]{1,0:T(8,128)(2,1)} %param.9) | copy-start | bytes 196612
Sparse Core Ops, SparseCore 0:
  105.1 30.9 reduce-scatter.1
